TPU v7x, 32 devices: a whole 2x2x4 slice. The times are simulated.
32 devices in a mesh: fsdp: 2 (over x), rep: 16 (over z, y, core).
Axes of the slice: x: 2, y: 2, z: 4, core: 2. Of those that a mesh axis runs over, the one named last changes fastest.
Arguments:
- images: bfloat16 [128, 197, 384], P(('fsdp', 'rep')), may hold values from -5 to 5
- cotangent: bfloat16 [128, 197, 384], P(('fsdp', 'rep')), may hold values from -6 to 6
- weights: float32 [1777664], P('fsdp'), may hold values from -3 to 3
- first_moment: float32 [1777664], P(('fsdp', 'rep'))
- second_moment: float32 [1777664], P(('fsdp', 'rep')), as said below
Outputs:
- output: bfloat16 [128, 197, 384], P(('fsdp', 'rep'))
- input_grad: bfloat16 [128, 197, 384], P(('fsdp', 'rep'))
- new_weights: float32 [1777664], P('fsdp')
- gradients: float32 [1777664], P(('fsdp', 'rep'))
- new_first: float32 [1777664], P(('fsdp', 'rep'))
- new_second: float32 [1777664], P(('fsdp', 'rep'))
Inputs may be any that keep to these rules, and one draw needn't show every extreme that they name: second_moment is positive.
All inputs are finite; a program needn't handle non-finite values.
Results may differ from a plain program's by a relative error of at most 0.0095.
The roundings to bfloat16 on the way count: a program that leaves them out, or rounds other values in their place, can miss the bound.
Values may be sent and summed in bfloat16 or wider, within the bound.
A program may use at most 128 MiB of HBM per device.

v0:
```python
import jax
import jax.numpy as jnp
from jax import lax
from jax.sharding import PartitionSpec as P

D = 384
H = 6
FF = 1536
norm_eps = 1e-06
half_root = 0.7071067811865476
inv_root_two_pi = 0.3989422804014327
beta_one = 0.9
beta_two = 0.999
learn_rate = 0.02
decay_rate = 0.05
adam_eps = 1e-08


def product(form, left, right):
    return jnp.einsum(form, left, right, preferred_element_type=jnp.float32)


def layer_norm_forward(values):
    centred = values - jnp.mean(values, -1, keepdims=True)
    variance = jnp.mean(centred * centred, -1, keepdims=True)
    inverse = lax.rsqrt(variance + norm_eps)
    return (centred * inverse, inverse)


def layer_norm_backward(d_scaled, scaled, inverse):
    first_mean = jnp.mean(d_scaled, -1, keepdims=True)
    second_mean = jnp.mean(d_scaled * scaled, -1, keepdims=True)
    return (d_scaled - first_mean - scaled * second_mean) * inverse


def unpack(flat_vec):
    edge_one = 3 * D * D
    edge_two = edge_one + D * D
    edge_three = edge_two + D * FF
    edge_four = edge_three + FF * D
    edge_five = edge_four + 8 * D
    w_qkv = flat_vec[:edge_one].reshape(D, 3 * D)
    w_proj = flat_vec[edge_one:edge_two].reshape(D, D)
    w_fc1 = flat_vec[edge_two:edge_three].reshape(D, FF)
    w_fc2 = flat_vec[edge_three:edge_four].reshape(FF, D)
    vectors = flat_vec[edge_four:edge_five].reshape(8, D)
    b_fc1 = flat_vec[edge_five : edge_five + FF]
    return (w_qkv, w_proj, w_fc1, w_fc2, vectors, b_fc1)


def pack(grads, length):
    pieces = [grad.reshape(-1) for grad in grads]
    used = sum((piece_arr.shape[0] for piece_arr in pieces))
    pieces.append(jnp.zeros((length - used,), jnp.float32))
    return jnp.concatenate(pieces)


def layer_block(images, cotangent, fwd_params, bwd_params):
    w_qkv, w_proj, w_fc1, w_fc2, vectors, b_fc1 = fwd_params
    back_qkv, back_proj, back_fc1, back_fc2, back_vectors, back_b1 = bwd_params
    batch, length, width = images.shape
    head_size = width // H
    token_rows = batch * length
    scale = head_size ** (-0.5)
    vector_float = vectors.astype(jnp.float32)
    backward_vector_slice = back_vectors.astype(jnp.float32)
    input_token_rows = images.astype(jnp.float32).reshape(token_rows, width)
    first_centered_scaled, first_inverse_deviation = layer_norm_forward(input_token_rows)
    first_normed_rows = (first_centered_scaled * vector_float[0] + vector_float[1]).astype(
        jnp.bfloat16
    )
    qkv_rows = jnp.dot(first_normed_rows, w_qkv, preferred_element_type=jnp.float32)
    query = (
        (qkv_rows[:, :width] + vector_float[2])
        .astype(jnp.bfloat16)
        .reshape(batch, length, H, head_size)
    )
    key_arr = (
        qkv_rows[:, width : 2 * width].astype(jnp.bfloat16).reshape(batch, length, H, head_size)
    )
    value = (
        (qkv_rows[:, 2 * width :] + vector_float[3])
        .astype(jnp.bfloat16)
        .reshape(batch, length, H, head_size)
    )
    scores = product("bqhd,bkhd->bhqk", query, key_arr) * scale
    top_score = jnp.max(scores, -1, keepdims=True)
    log_total = top_score + jnp.log(jnp.sum(jnp.exp(scores - top_score), -1, keepdims=True))
    probs_bf = jnp.exp(scores - log_total).astype(jnp.bfloat16)
    mixed = (
        product("bhqk,bkhd->bqhd", probs_bf, value).astype(jnp.bfloat16).reshape(token_rows, width)
    )
    residual_stream = (
        input_token_rows
        + jnp.dot(mixed, w_proj, preferred_element_type=jnp.float32)
        + vector_float[4]
    )
    second_centered_scaled, second_inverse_deviation = layer_norm_forward(residual_stream)
    second_normed_rows = (second_centered_scaled * vector_float[5] + vector_float[6]).astype(
        jnp.bfloat16
    )
    preact = jnp.dot(second_normed_rows, w_fc1, preferred_element_type=jnp.float32) + b_fc1.astype(
        jnp.float32
    )
    normal_cdf = 0.5 * (1.0 + jax.scipy.special.erf(preact * half_root))
    activ = (preact * normal_cdf).astype(jnp.bfloat16)
    result = (
        residual_stream
        + jnp.dot(activ, w_fc2, preferred_element_type=jnp.float32)
        + vector_float[7]
    )
    d_out = cotangent.reshape(token_rows, width)
    output_gradient_float = d_out.astype(jnp.float32)
    grad_fc2 = jnp.dot(activ.T, d_out, preferred_element_type=jnp.float32)
    grad_bias2 = jnp.sum(output_gradient_float, 0)
    d_act = jnp.dot(d_out, back_fc2.T, preferred_element_type=jnp.float32)
    d_pre = d_act * (normal_cdf + preact * jnp.exp(-0.5 * preact * preact) * inv_root_two_pi)
    grad_bias1 = jnp.sum(d_pre, 0)
    d_pre_bf = d_pre.astype(jnp.bfloat16)
    grad_fc1 = jnp.dot(second_normed_rows.T, d_pre_bf, preferred_element_type=jnp.float32)
    second_norm_gradient = jnp.dot(d_pre_bf, back_fc1.T, preferred_element_type=jnp.float32)
    gain2_gradient = jnp.sum(second_norm_gradient * second_centered_scaled, 0)
    grad_shift2 = jnp.sum(second_norm_gradient, 0)
    residual_gradient = output_gradient_float + layer_norm_backward(
        second_norm_gradient * backward_vector_slice[5],
        second_centered_scaled,
        second_inverse_deviation,
    )
    grad_pbias = jnp.sum(residual_gradient, 0)
    d_resid_bf = residual_gradient.astype(jnp.bfloat16)
    grad_proj = jnp.dot(mixed.T, d_resid_bf, preferred_element_type=jnp.float32)
    d_mixed = jnp.dot(d_resid_bf, back_proj.T, preferred_element_type=jnp.float32)
    d_mixed = d_mixed.astype(jnp.bfloat16).reshape(batch, length, H, head_size)
    scores_again = product("bqhd,bkhd->bhqk", query, key_arr) * scale
    probs_full = jnp.exp(scores_again - log_total)
    probs_again = probs_full.astype(jnp.bfloat16)
    d_probs = product("bqhd,bkhd->bhqk", d_mixed, value)
    d_value = product("bhqk,bqhd->bkhd", probs_again, d_mixed).reshape(token_rows, width)
    delta = jnp.sum(probs_full * d_probs, -1, keepdims=True)
    d_scores = (probs_full * (d_probs - delta) * scale).astype(jnp.bfloat16)
    d_query = product("bhqk,bkhd->bqhd", d_scores, key_arr).reshape(token_rows, width)
    d_key = product("bhqk,bqhd->bkhd", d_scores, query).reshape(token_rows, width)
    grad_qbias = jnp.sum(d_query, 0)
    grad_vbias = jnp.sum(d_value, 0)
    d_qkv = jnp.concatenate([d_query, d_key, d_value], 1).astype(jnp.bfloat16)
    grad_qkv = jnp.dot(first_normed_rows.T, d_qkv, preferred_element_type=jnp.float32)
    first_norm_gradient = jnp.dot(d_qkv, back_qkv.T, preferred_element_type=jnp.float32)
    gain1_gradient = jnp.sum(first_norm_gradient * first_centered_scaled, 0)
    grad_shift1 = jnp.sum(first_norm_gradient, 0)
    input_gradient = residual_gradient + layer_norm_backward(
        first_norm_gradient * backward_vector_slice[0],
        first_centered_scaled,
        first_inverse_deviation,
    )
    grad_vectors = jnp.stack(
        [
            gain1_gradient,
            grad_shift1,
            grad_qbias,
            grad_vbias,
            grad_pbias,
            gain2_gradient,
            grad_shift2,
            grad_bias2,
        ]
    )
    grads = (grad_qkv, grad_proj, grad_fc1, grad_fc2, grad_vectors, grad_bias1)
    out_block = result.astype(jnp.bfloat16).reshape(batch, length, width)
    input_block = input_gradient.astype(jnp.bfloat16).reshape(batch, length, width)
    return (out_block, input_block, grads)


def adamw(weight_vals, grad_vals, first_vals, second_vals):
    first_new = beta_one * first_vals + (1.0 - beta_one) * grad_vals
    second_new = beta_two * second_vals + (1.0 - beta_two) * grad_vals * grad_vals
    first_hat = first_new / (1.0 - beta_one**2)
    second_hat = second_new / (1.0 - beta_two**2)
    updated = weight_vals - learn_rate * (
        first_hat / (jnp.sqrt(second_hat) + adam_eps) + decay_rate * weight_vals
    )
    return (updated, first_new, second_new)


def on_device(images, cotangent, weights, first_moment, second_moment):
    half_bf = weights.astype(jnp.bfloat16)
    params = unpack(lax.all_gather(half_bf, "fsdp", axis=0, tiled=True))
    back_params = unpack(lax.all_gather(half_bf, "fsdp", axis=0, tiled=True))
    output, input_grad, grads = layer_block(images, cotangent, params, back_params)
    flat_grad = pack(grads, 2 * weights.shape[0])
    half_grad = lax.psum_scatter(
        flat_grad.astype(jnp.bfloat16), "fsdp", scatter_dimension=0, tiled=True
    ).astype(jnp.float32)
    piece_len = first_moment.shape[0]
    offset = lax.axis_index("rep") * piece_len
    summed_all = lax.psum(half_grad, "rep")
    own_grad = lax.dynamic_slice_in_dim(summed_all, offset, piece_len)
    own_weights = lax.dynamic_slice_in_dim(weights, offset, piece_len)
    new_own, new_first, new_second = adamw(own_weights, own_grad, first_moment, second_moment)
    new_weights = lax.all_gather(new_own, "rep", axis=0, tiled=True)
    return (output, input_grad, new_weights, own_grad, new_first, new_second)


def solution(mesh):
    in_specs = (
        P(("fsdp", "rep"), None, None),
        P(("fsdp", "rep"), None, None),
        P("fsdp"),
        P(("fsdp", "rep")),
        P(("fsdp", "rep")),
    )
    out_specs = (
        P(("fsdp", "rep"), None, None),
        P(("fsdp", "rep"), None, None),
        P("fsdp"),
        P(("fsdp", "rep")),
        P(("fsdp", "rep")),
        P(("fsdp", "rep")),
    )
    return jax.shard_map(
        on_device, mesh=mesh, in_specs=in_specs, out_specs=out_specs, check_vma=False
    )
```

profile of v0, /device:TPU:0, one launch (start us, length us, event | category | flops | bytes accessed | tf_op | source)
XLA Modules:
  0.0 480.9 jit_solution(8858606511135499291)
XLA Ops:
  7.2 3.4 convert_element_type.75
  12.6 1.1 copy.81
  17.3 1.4 reshape.202
  18.8 44.2 %all-gather.4.cloned.1.call-done = bf16[1777664]{0:T(1024)(128)(2,1)} async-done(((bf16[888832]{0:T(1024)(128)(2,1)}), bf16[1777664]{0:T(1024)(128)(2,1)}) %all-gather.4.cloned.1.call-update) | async-done | bytes 3555344 | tf_op jit(solution)/shard_map/all_gather | solution.py:186
  66.9 1.2 convert_element_type.78
  68.2 1.9 reshape.203
  70.1 2.8 fusion.60
  72.9 3.4 reshape.210
  76.4 2.2 reshape.209
  78.6 2.4 fusion.66
  82.1 2.0 reshape.227
  84.1 1.9 copy.90
  86.0 3.3 reshape.228
  89.2 2.7 copy.91
  91.9 2.0 reshape.226
  93.9 1.9 copy.92
  95.8 2.0 multiply_reduce_fusion.1
  98.8 1.2 copy-done
  100.0 1.1 fusion.30
  101.1 1.5 copy.94
  102.6 2.7 reshape.207
  105.3 2.0 fusion.62
  107.7 4.7 multiply_convert_fusion.1
  112.4 16.3 %fusion.65 = (bf16[1536]{0:T(1024)(128)(2,1)}, bf16[788,1536]{1,0:T(8,128)(2,1)S(1)}) fusion(f32[788,1536]{1,0:T(8,128)S(1)} %get-tuple-element.61, f32[1536]{0:T(1024)S(1)} %slice_convert_fusion.2, bf16[788,384]{1,0:T(8,128)(2,1)S(1)} %copy-done.13, bf16[1536,384]{1,0:T(8,128)(2,1)S(1)} %copy-done.18), kind=kOutput, calls=%fused_computation.106 | convolution fusion | flops 944085504 | bytes 9056256 | tf_op jit(solution)/shard_map/dot_general | solution.py:116
  128.8 2.2 multiply_reduce_fusion.2
  131.0 2.6 convolution_convert_fusion.1
  134.7 1.2 convolution_convert_fusion.5
  136.0 1.4 convolution_convert_fusion.4
  137.4 3.0 reshape.229
  140.4 2.6 copy.97
  143.1 5.1 %bitcast_convert_fusion = (bf16[4,197,6,64]{1,3,2,0:T(8,128)(2,1)}, f32[4,6,64,197]{3,2,1,0:T(8,128)}) fusion(bf16[4,197,6,64]{1,3,2,0:T(8,128)(2,1)} %copy.97, f32[4,6,197,197]{2,3,1,0:T(8,128)} %copy-done, f32[4,6,197]{2,1,0:T(8,128)S(1)} %log_add_fusion), kind=kOutput, calls=%fused_computation.27 | convolution fusion | flops 122318088 | bytes 6165312 | tf_op jit(solution)/shard_map/bhqk,bqhd->bkhd/dot_general | solution.py:20
  148.2 3.1 fusion.67
  151.3 10.3 %fusion.31 = bf16[4,197,6,64]{1,3,2,0:T(8,128)(2,1)} fusion(bf16[4,197,6,64]{1,3,2,0:T(8,128)(2,1)} %copy-done.11, f32[4,6,197,197]{2,3,1,0:T(8,128)} %fusion.67, f32[4,6,197,197]{2,3,1,0:T(8,128)} %copy-done, f32[4,6,197]{2,1,0:T(8,128)S(1)} %log_add_fusion), kind=kOutput, calls=%fused_computation.39 | convolution fusion | flops 127911504 | bytes 8680608 | tf_op jit(solution)/shard_map/bhqk,bqhd->bkhd/dot_general | solution.py:20
  161.6 10.5 %bitcast_convert_fusion.1 = (bf16[4,197,6,64]{1,3,2,0:T(8,128)(2,1)}, f32[4,6,64,197]{3,2,1,0:T(8,128)}) fusion(bf16[4,197,6,64]{1,3,2,0:T(8,128)(2,1)S(1)} %copy-done.12, f32[4,6,197,197]{2,3,1,0:T(8,128)} %fusion.67, f32[4,6,197,197]{2,3,1,0:T(8,128)} %copy-done, f32[4,6,197]{2,1,0:T(8,128)S(1)} %log_add_fusion), kind=kOutput, calls=%fused_computation.29 | convolution fusion | flops 127911504 | bytes 9890976 | tf_op jit(solution)/shard_map/bhqk,bkhd->bqhd/dot_general | solution.py:20
  172.1 1.7 copy.107
  173.9 1.4 reshape.216
  175.3 1.7 copy.101
  177.1 1.5 reshape.214
  178.5 1.7 copy.104
  180.3 1.4 reshape.215
  181.7 1.3 constant_dynamic-update-slice_fusion.2
  183.0 1.2 constant_dynamic-update-slice_fusion.1
  184.2 1.2 constant_dynamic-update-slice_fusion
  185.5 2.8 multiply_reduce_fusion.3
  188.3 2.6 convolution_convert_fusion.2
  190.9 2.8 convolution_convert_fusion
  193.8 3.1 reshape.221
  196.9 3.5 reshape.220
  201.2 1.6 bitcast_reduce_fusion
  202.9 1.6 bitcast_reduce_fusion.1
  204.6 2.1 reshape.218
  207.7 1.7 constant_dynamic-update-slice_fusion.7
  209.4 1.1 constant_dynamic-update-slice_fusion.6
  210.5 1.1 constant_dynamic-update-slice_fusion.5
  212.2 1.4 dynamic-update-slice.5
  213.7 1.4 dynamic-update-slice.6
  216.4 93.6 %all-reduce.6.cloned.1.call-done = bf16[1777664]{0:T(1024)(128)(2,1)} async-done(((bf16[1777664]{0:T(1024)(128)(2,1)}), bf16[1777664]{0:T(1024)(128)(2,1)}) %all-reduce.6.cloned.1.call-update) | async-done | bytes 3555344
  310.0 3.5 dynamic-slice_convert_fusion
  313.6 107.2 %all-reduce.4.cloned.1.call-done = f32[888832]{0:T(1024)} async-done(((f32[888832]{0:T(1024)}), f32[888832]{0:T(1024)}) %all-reduce.4.cloned.1.call-update) | async-done | bytes 3555344 | tf_op jit(solution)/shard_map/psum | solution.py:195
  420.8 2.1 multiply_subtract_fusion
  423.7 4.3 fusion.29
  428.0 1.3 reshape.211
  432.6 37.5 %all-gather.6.cloned.1.call-done = f32[16,1,55552]{2,1,0:T(1,128)} async-done(((f32[1,1,55552]{2,1,0:T(1,128)}), f32[16,1,55552]{2,1,0:T(1,128)}) %all-gather.6.cloned.1.call-update) | async-done | bytes 3555344 | tf_op jit(solution)/shard_map/all_gather | solution.py:199
  470.1 4.0 copy.135
  (128 shorter events, 20.6 us)
Async XLA Ops:
  7.2 55.9 %all-gather.4.cloned.1.call-start = ((), (), s32[]{:S(2)}) async-start(), calls=%async_computation | async-start | bytes 5332992 | tf_op jit(solution)/shard_map/all_gather | solution.py:186
  10.6 1.1 copy-start.15
  10.6 2.0 copy-start.4
  10.6 299.4 %all-reduce.6.cloned.1.call-start = ((), (), s32[]{:S(2)}) async-start(), calls=%async_computation.3 | async-start | bytes 7110656
  18.8 86.6 %copy-start.1 = (f32[788,384]{1,0:T(8,128)}, f32[788,384]{1,0:T(8,128)S(1)}, u32[]{:S(2)}) copy-start(f32[788,384]{1,0:T(8,128)S(1)} %reshape.202) | copy-start | bytes 3631108
  64.3 3.9 copy-start.22
  64.3 3.9 copy-start.26
  66.0 2.2 slice-start
  86.0 9.9 %copy-start.11 = (bf16[4,197,6,64]{1,3,2,0:T(8,128)(2,1)}, bf16[4,197,6,64]{1,3,2,0:T(8,128)(2,1)S(1)}, u32[]{:S(2)}) copy-start(bf16[4,197,6,64]{1,3,2,0:T(8,128)(2,1)S(1)} %copy.90) | copy-start | bytes 1815556
  97.8 2.2 copy-start
  105.3 2.3 copy-start.9
  107.7 4.7 copy-start.13
  107.7 4.7 copy-start.18
  112.4 16.3 %copy-start.19 = (bf16[384,1536]{1,0:T(8,128)(2,1)S(1)}, bf16[384,1536]{1,0:T(8,128)(2,1)}, u32[]{:S(2)}) copy-start(bf16[384,1536]{1,0:T(8,128)(2,1)} %reshape.209) | copy-start | bytes 3538948
  133.6 1.1 copy-start.6
  143.1 5.1 %copy-start.5 = (bf16[4,197,6,64]{1,3,2,0:T(8,128)(2,1)S(1)}, bf16[4,197,6,64]{1,3,2,0:T(8,128)(2,1)}, u32[]{:S(2)}) copy-start(bf16[4,197,6,64]{1,3,2,0:T(8,128)(2,1)} %copy.97) | copy-start | bytes 1815556
  151.3 10.3 %copy-start.12 = (bf16[4,197,6,64]{1,3,2,0:T(8,128)(2,1)S(1)}, bf16[4,197,6,64]{1,3,2,0:T(8,128)(2,1)}, u32[]{:S(2)}) copy-start(bf16[4,197,6,64]{1,3,2,0:T(8,128)(2,1)} %copy.91) | copy-start | bytes 1815556
  181.7 3.7 copy-start.2
  181.7 3.7 copy-start.10
  181.7 3.7 copy-start.23
  181.7 3.7 copy-start.24
  181.7 3.7 copy-start.25
  185.5 2.8 copy-start.27
  188.3 2.6 copy-start.14
  188.3 2.6 copy-start.34
  193.8 6.6 %copy-start.32 = (bf16[384]{0:T(512)(128)(2,1)S(1)}, bf16[384]{0:T(512)(128)(2,1)}, u32[]{:S(2)}) copy-start(bf16[384]{0:T(512)(128)(2,1)} %get-tuple-element.30) | copy-start | bytes 2308
  193.8 6.6 %copy-start.31 = (bf16[384]{0:T(512)(128)(2,1)S(1)}, bf16[384]{0:T(512)(128)(2,1)}, u32[]{:S(2)}) copy-start(bf16[384]{0:T(512)(128)(2,1)} %get-tuple-element.36) | copy-start | bytes 2308
  193.8 6.6 %copy-start.17 = (bf16[384,384]{1,0:T(8,128)(2,1)S(1)}, bf16[384,384]{1,0:T(8,128)(2,1)}, u32[]{:S(2)}) copy-start(bf16[384,384]{1,0:T(8,128)(2,1)} %convolution_convert_fusion.5) | copy-start | bytes 884740
  202.8 3.8 copy-start.28
  206.7 2.7 copy-start.8
  206.7 3.8 copy-start.7
  209.4 2.8 copy-start.29
  211.6 3.5 copy-start.33
  215.1 205.7 %all-reduce.4.cloned.1.call-start = ((), (), s32[]{:S(2)}) async-start(), calls=%async_computation.1 | async-start | bytes 7110656 | tf_op jit(solution)/shard_map/psum | solution.py:195
  313.5 107.3 %copy-start.20 = (f32[55552]{0:T(1024)S(1)}, f32[55552]{0:T(1024)}, u32[]{:S(2)}) copy-start(f32[55552]{0:T(1024)} %param.8) | copy-start | bytes 666628
  313.5 107.3 %copy-start.21 = (f32[55552]{0:T(1024)S(1)}, f32[55552]{0:T(1024)}, u32[]{:S(2)}) copy-start(f32[55552]{0:T(1024)} %param.9) | copy-start | bytes 666628
  313.5 110.2 %copy-start.30 = (f32[384]{0:T(512)S(1)}, f32[384]{0:T(512)}, u32[]{:S(2)}) copy-start(f32[384]{0:T(512)} %get-tuple-element.48) | copy-start | bytes 4612
  313.5 156.6 %all-gather.6.cloned.1.call-start = ((), (), s32[]{:S(2)}) async-start(), calls=%async_computation.2 | async-start | bytes 3777536 | tf_op jit(solution)/shard_map/all_gather | solution.py:199
  428.0 2.4 copy-start.3
  429.3 1.6 copy-start.16
Sparse Core Ops, SparseCore 0:
  10.8 52.2 all-gather.3
  215.2 94.7 all-reduce.5
  314.2 106.4 all-reduce.3
  423.8 46.2 all-gather.5
where the time goes:
time: 486 us; the launch traced here: 481 us
  waiting for transfers between devices  283 us (58%)
  local copies, waits for them, and re-layouts  88.2 us (18%)
  matrix products  77.6 us (16%)
  other arithmetic  17.2 us (4%)
  between operations  15.1 us (3%)
    psum x1, waiting for transfers between devices, on_device(): summed_all = lax.psum(half_grad, 'rep')  107 us
    unnamed x5, waiting for transfers between devices  93.7 us
    all_gather x1, waiting for transfers between devices, on_device(): params = unpack(lax.all_gather(half_bf, 'fsdp', axis=0, tiled=True))  44.2 us
    all_gather x1, waiting for transfers between devices, on_device(): new_weights = lax.all_gather(new_own, 'rep', axis=0, tiled=True)  37.5 us
    dot_general x6, matrix products, product(): return jnp.einsum(form, left, right, preferred_element_type=jnp.float32)  32.1 us
    unnamed x86, local copies, waits for them, and re-layouts  20.6 us
    dot_general x1, matrix products, layer_block(): d_act = jnp.dot(d_out, back_fc2.T, preferred_element_type=jnp.float32)  16.3 us
  transfers between devices with their start and end apart: 4, of which 4 were waited for; matrix products, arithmetic and copies ran while one was open for 3% of the time, Pallas kernels for 0%

commit v1 on v0

--- a/solution.py
+++ b/solution.py
@@ -196,7 +196,14 @@
     own_grad = lax.dynamic_slice_in_dim(summed_all, offset, piece_len)
     own_weights = lax.dynamic_slice_in_dim(weights, offset, piece_len)
     new_own, new_first, new_second = adamw(own_weights, own_grad, first_moment, second_moment)
-    new_weights = lax.all_gather(new_own, "rep", axis=0, tiled=True)
+    ways = lax.axis_size("rep")
+    pieces_2 = [new_own]
+    for far in range(1, ways):
+        pieces_2.append(
+            lax.ppermute(pieces_2[far - 1], "rep", [(d, (d - 1) % ways) for d in range(ways)])
+        )
+    line = jnp.concatenate(pieces_2, axis=0)
+    new_weights = jnp.roll(line, lax.axis_index("rep") * new_own.shape[0], axis=0)
     return (output, input_grad, new_weights, own_grad, new_first, new_second)
 
 

time: 486 us -> 585 us (1.20)
  starting transfers between devices: 0.16 us -> 62.4 us
  local copies, waits for them, and re-layouts: 88.2 us -> 141 us
  waiting for transfers between devices: 283 us -> 269 us
  matrix products: 77.6 us -> 70.2 us
    ppermute x0 -> x15, starting transfers between devices: none -> 62.3 us  [on_device(): lax.ppermute(pieces_2[far - 1], 'rep', [(d, (d - 1) % ways) for d in rang...]
    unnamed x86 -> x128, local copies, waits for them, and re-layouts: 20.6 us -> 65.1 us
    all_gather x1 -> x0, waiting for transfers between devices: 37.5 us -> none  [on_device(): new_weights = lax.all_gather(new_own, 'rep', axis=0, tiled=True)]
    ppermute x0 -> x15, waiting for transfers between devices: none -> 22.8 us  [on_device(): lax.ppermute(pieces_2[far - 1], 'rep', [(d, (d - 1) % ways) for d in rang...]
    dot_general x1, matrix products: 16.3 us -> 4.45 us  [layer_block(): d_act = jnp.dot(d_out, back_fc2.T, preferred_element_type=jnp.float32)]
    unnamed x5 -> x4, waiting for transfers between devices: 93.7 us -> 93.6 us
  transfers between devices with their start and end apart: 4 -> 18, of which waited for: 4 -> 15; matrix products, arithmetic and copies ran while one was open for 3% -> 7% of each run, Pallas kernels for 0% -> 0%
where the time goes in v1:
time: 585 us; the launch traced here: 578 us
  waiting for transfers between devices  269 us (46%)
  local copies, waits for them, and re-layouts  141 us (24%)
  matrix products  70.2 us (12%)
  starting transfers between devices  62.4 us (11%)
  other arithmetic  20.5 us (4%)
  between operations  15.1 us (3%)
    psum x1, waiting for transfers between devices, on_device(): summed_all = lax.psum(half_grad, 'rep')  107 us
    unnamed x4, waiting for transfers between devices  93.6 us
    unnamed x128, local copies, waits for them, and re-layouts  65.1 us
    ppermute x15, starting transfers between devices, on_device(): lax.ppermute(pieces_2[far - 1], 'rep', [(d, (d - 1) % ways) for d in rang...  62.3 us
    all_gather x1, waiting for transfers between devices, on_device(): params = unpack(lax.all_gather(half_bf, 'fsdp', axis=0, tiled=True))  45 us
    dot_general x6, matrix products, product(): return jnp.einsum(form, left, right, preferred_element_type=jnp.float32)  33.2 us
    ppermute x15, waiting for transfers between devices, on_device(): lax.ppermute(pieces_2[far - 1], 'rep', [(d, (d - 1) % ways) for d in rang...  22.8 us
  transfers between devices with their start and end apart: 18, of which 15 were waited for; matrix products, arithmetic and copies ran while one was open for 7% of the time, Pallas kernels for 0%

profile of v1, /device:TPU:0, one launch (start us, length us, event | category | flops | bytes accessed | tf_op | source)
XLA Modules:
  0.0 577.5 jit_solution(16406666578554254514)
XLA Ops:
  7.2 3.4 convert_element_type.75
  18.1 45.0 %all-gather.2.cloned.1.call-done = bf16[1777664]{0:T(1024)(128)(2,1)} async-done(((bf16[888832]{0:T(1024)(128)(2,1)}), bf16[1777664]{0:T(1024)(128)(2,1)}) %all-gather.2.cloned.1.call-update) | async-done | bytes 3555344 | tf_op jit(solution)/shard_map/all_gather | solution.py:186
  67.2 1.9 reshape.203
  69.2 2.4 fusion.66
  72.6 2.0 reshape.224
  74.7 2.0 copy.92
  76.7 2.0 reshape.225
  78.7 1.9 copy.90
  80.7 3.3 reshape.226
  83.9 2.6 copy.91
  86.5 2.0 multiply_reduce_fusion.1
  93.6 2.8 fusion.60
  96.5 2.2 reshape.209
  100.8 2.3 reshape.210
  103.8 4.6 multiply_convert_fusion.1
  108.5 4.4 fusion.65
  112.9 2.2 multiply_reduce_fusion.2
  117.7 3.0 reshape.227
  120.7 2.7 copy.97
  123.4 4.2 fusion.67
  127.6 10.7 %bitcast_convert_fusion.1 = (bf16[4,197,6,64]{1,3,2,0:T(8,128)(2,1)}, f32[4,6,64,197]{3,2,1,0:T(8,128)}) fusion(bf16[4,197,6,64]{1,3,2,0:T(8,128)(2,1)} %copy.91, f32[4,6,197,197]{2,3,1,0:T(8,128)} %fusion.67, f32[4,6,197,197]{2,3,1,0:T(8,128)} %copy-done, f32[4,6,197]{2,1,0:T(8,128)S(1)} %log_add_fusion), kind=kOutput, calls=%fused_computation.29 | convolution fusion | flops 127911504 | bytes 9890976 | tf_op jit(solution)/shard_map/bhqk,bkhd->bqhd/dot_general | solution.py:20
  138.3 10.2 %fusion.31 = bf16[4,197,6,64]{1,3,2,0:T(8,128)(2,1)} fusion(bf16[4,197,6,64]{1,3,2,0:T(8,128)(2,1)} %copy-done.8, f32[4,6,197,197]{2,3,1,0:T(8,128)} %fusion.67, f32[4,6,197,197]{2,3,1,0:T(8,128)} %copy-done, f32[4,6,197]{2,1,0:T(8,128)S(1)} %log_add_fusion), kind=kOutput, calls=%fused_computation.39 | convolution fusion | flops 127911504 | bytes 8680608 | tf_op jit(solution)/shard_map/bhqk,bqhd->bkhd/dot_general | solution.py:20
  148.5 5.0 bitcast_convert_fusion
  155.6 2.0 constant_dynamic-update-slice_fusion.2
  157.6 2.6 copy.104
  160.2 3.1 reshape.215
  163.3 2.6 copy.107
  166.0 2.7 reshape.216
  168.7 2.0 constant_dynamic-update-slice_fusion.1
  170.7 2.0 constant_dynamic-update-slice_fusion
  172.8 4.8 multiply_reduce_fusion.3
  177.6 2.6 convolution_convert_fusion.2
  181.5 2.6 convolution_convert_fusion.1
  184.1 2.0 reshape.218
  188.2 3.5 reshape.220
  191.7 4.6 convolution_convert_fusion
  196.3 3.2 reshape.221
  203.8 2.4 constant_dynamic-update-slice_fusion.7
  212.0 93.6 %all-reduce.6.cloned.1.call-done = bf16[1777664]{0:T(1024)(128)(2,1)} async-done(((bf16[1777664]{0:T(1024)(128)(2,1)}), bf16[1777664]{0:T(1024)(128)(2,1)}) %all-reduce.6.cloned.1.call-update) | async-done | bytes 3555344
  305.6 3.5 dynamic-slice_convert_fusion
  309.1 107.2 %all-reduce.4.cloned.1.call-done = f32[888832]{0:T(1024)} async-done(((f32[888832]{0:T(1024)}), f32[888832]{0:T(1024)}) %all-reduce.4.cloned.1.call-update) | async-done | bytes 3555344 | tf_op jit(solution)/shard_map/psum | solution.py:195
  416.3 2.2 constant_dynamic-update-slice_fusion.4
  419.1 3.5 collective-permute-done
  422.6 4.6 collective-permute-start.1
  427.2 3.5 collective-permute-done.1
  430.7 4.6 collective-permute-start.2
  435.4 3.5 collective-permute-done.2
  438.8 4.6 collective-permute-start.3
  443.5 3.5 collective-permute-done.3
  446.9 4.7 collective-permute-start.4
  451.7 4.3 fusion.29
  460.1 3.8 collective-permute-done.5
  463.9 4.5 collective-permute-start.6
  468.4 3.5 collective-permute-done.6
  471.9 4.7 collective-permute-start.7
  476.6 2.2 add_convert_fusion.1
  480.4 4.6 collective-permute-start.8
  488.8 4.5 collective-permute-start.9
  496.8 4.6 collective-permute-start.10
  504.9 4.6 collective-permute-start.11
  513.0 4.6 collective-permute-start.12
  521.1 4.6 collective-permute-start.13
  529.2 4.6 collective-permute-start.14
  566.0 4.8 dynamic_slice.12
  (201 shorter events, 97.6 us)
Async XLA Ops:
  7.2 3.6 copy-start.3
  7.2 55.9 %all-gather.2.cloned.1.call-start = ((), (), s32[]{:S(2)}) async-start(), calls=%async_computation | async-start | bytes 5332992 | tf_op jit(solution)/shard_map/all_gather | solution.py:186
  10.7 2.7 copy-start.13
  10.7 294.9 %all-reduce.6.cloned.1.call-start = ((), (), s32[]{:S(2)}) async-start(), calls=%async_computation.2 | async-start | bytes 7110656
  13.3 85.3 %copy-start.1 = (f32[788,384]{1,0:T(8,128)}, f32[788,384]{1,0:T(8,128)S(1)}, u32[]{:S(2)}) copy-start(f32[788,384]{1,0:T(8,128)S(1)} %reshape.202) | copy-start | bytes 3631108
  63.1 4.1 slice-start
  64.5 0.6 copy-start.33
  64.5 4.7 copy-start.29
  80.6 7.9 %copy-start.8 = (bf16[4,197,6,64]{1,3,2,0:T(8,128)(2,1)}, bf16[4,197,6,64]{1,3,2,0:T(8,128)(2,1)S(1)}, u32[]{:S(2)}) copy-start(bf16[4,197,6,64]{1,3,2,0:T(8,128)(2,1)S(1)} %copy.90) | copy-start | bytes 1815556
  88.6 2.2 copy-start
  89.5 3.3 slice-start.1
  93.6 5.0 copy-start.9
  103.1 5.3 copy-start.14
  103.8 4.6 copy-start.12
  108.4 4.5 copy-start.15
  108.4 4.5 copy-start.26
  112.9 2.2 copy-start.10
  138.3 10.3 %copy-start.4 = (bf16[4,197,6,64]{1,3,2,0:T(8,128)(2,1)S(1)}, bf16[4,197,6,64]{1,3,2,0:T(8,128)(2,1)}, u32[]{:S(2)}) copy-start(bf16[4,197,6,64]{1,3,2,0:T(8,128)(2,1)} %copy.97) | copy-start | bytes 1815556
  148.5 5.0 copy-start.22
  160.2 12.5 %copy-start.7 = (bf16[384,1152]{1,0:T(8,128)(2,1)S(1)}, bf16[384,1152]{1,0:T(8,128)(2,1)}, u32[]{:S(2)}) copy-start(bf16[384,1152]{1,0:T(8,128)(2,1)} %reshape.203) | copy-start | bytes 2654212
  160.2 12.5 %copy-start.30 = (f32[384]{0:T(512)S(1)}, f32[384]{0:T(512)}, u32[]{:S(2)}) copy-start(f32[384]{0:T(512)} %copy-done.29) | copy-start | bytes 4612
  160.2 12.5 %copy-start.31 = (f32[788]{0:T(1024)S(1)}, f32[788]{0:T(1024)}, u32[]{:S(2)}) copy-start(f32[788]{0:T(1024)} %rsqrt.22) | copy-start | bytes 9460
  160.2 12.5 %copy-start.32 = (f32[788]{0:T(1024)S(1)}, f32[788]{0:T(1024)}, u32[]{:S(2)}) copy-start(f32[788]{0:T(1024)} %div.48) | copy-start | bytes 9460
  172.7 4.8 copy-start.2
  172.8 4.8 copy-start.23
  172.8 4.8 copy-start.34
  177.5 2.7 copy-start.5
  177.6 3.9 copy-start.11
  177.6 3.9 copy-start.27
  177.6 3.9 copy-start.28
  196.3 6.6 %copy-start.36 = (bf16[384]{0:T(512)(128)(2,1)S(1)}, bf16[384]{0:T(512)(128)(2,1)}, u32[]{:S(2)}) copy-start(bf16[384]{0:T(512)(128)(2,1)} %get-tuple-element.43) | copy-start | bytes 2308
  196.3 6.6 %copy-start.40 = (bf16[384]{0:T(512)(128)(2,1)S(1)}, bf16[384]{0:T(512)(128)(2,1)}, u32[]{:S(2)}) copy-start(bf16[384]{0:T(512)(128)(2,1)} %get-tuple-element.30) | copy-start | bytes 2308
  196.3 6.6 %copy-start.39 = (bf16[384]{0:T(512)(128)(2,1)S(1)}, bf16[384]{0:T(512)(128)(2,1)}, u32[]{:S(2)}) copy-start(bf16[384]{0:T(512)(128)(2,1)} %get-tuple-element.36) | copy-start | bytes 2308
  196.3 6.6 %copy-start.35 = (bf16[1,384]{1,0:T(2,128)(2,1)S(1)}, bf16[1,384]{1,0:T(2,128)(2,1)}, u32[]{:S(2)}) copy-start(bf16[1,384]{1,0:T(2,128)(2,1)} %stack.43) | copy-start | bytes 2308
  201.2 6.7 %copy-start.37 = (bf16[1536]{0:T(1024)(128)(2,1)S(1)}, bf16[1536]{0:T(1024)(128)(2,1)}, u32[]{:S(2)}) copy-start(bf16[1536]{0:T(1024)(128)(2,1)} %get-tuple-element.69) | copy-start | bytes 9220
  203.0 3.1 copy-start.6
  206.2 4.6 copy-start.41
  210.7 205.6 %all-reduce.4.cloned.1.call-start = ((), (), s32[]{:S(2)}) async-start(), calls=%async_computation.1 | async-start | bytes 7110656 | tf_op jit(solution)/shard_map/psum | solution.py:195
  212.0 204.3 %copy-start.24 = (f32[55552]{0:T(1024)S(1)}, f32[55552]{0:T(1024)}, u32[]{:S(2)}) copy-start(f32[55552]{0:T(1024)} %param.8) | copy-start | bytes 666628
  212.0 204.3 %copy-start.25 = (f32[55552]{0:T(1024)S(1)}, f32[55552]{0:T(1024)}, u32[]{:S(2)}) copy-start(f32[55552]{0:T(1024)} %param.9) | copy-start | bytes 666628
  309.1 142.6 %copy-start.38 = (f32[384]{0:T(512)S(1)}, f32[384]{0:T(512)}, u32[]{:S(2)}) copy-start(f32[384]{0:T(512)} %get-tuple-element.49) | copy-start | bytes 4612
  418.6 4.1 collective-permute-start
  422.6 8.1 %collective-permute-start.1 = (f32[55552]{0:T(1024)S(1)}, f32[55552]{0:T(1024)S(1)}, u32[]{:S(2)}, u32[]{:S(2)}) collective-permute-start(f32[55552]{0:T(1024)S(1)} %collective-permute-done), channel_id=1, source_target_pairs={{0,15},{1,0},{2,1},{3,2},{4,3},{5,4},{6,5},{7,6},{8,7},{9,8},{10,9... | collective-permute-start | bytes 666632 | tf_op jit(solution)/shard_map/ppermute | solution.py:203
  430.7 25.2 %copy-start.16 = (f32[55552]{0:T(1024)}, f32[55552]{0:T(1024)S(1)}, u32[]{:S(2)}) copy-start(f32[55552]{0:T(1024)S(1)} %collective-permute-done.1) | copy-start | bytes 666628
  430.7 8.1 %collective-permute-start.2 = (f32[55552]{0:T(1024)S(1)}, f32[55552]{0:T(1024)S(1)}, u32[]{:S(2)}, u32[]{:S(2)}) collective-permute-start(f32[55552]{0:T(1024)S(1)} %collective-permute-done.1), channel_id=1, source_target_pairs={{0,15},{1,0},{2,1},{3,2},{4,3},{5,4},{6,5},{7,6},{8,7},{9,8},{10,9... | collective-permute-start | bytes 666632 | tf_op jit(solution)/shard_map/ppermute | solution.py:203
  438.8 17.1 %copy-start.18 = (f32[55552]{0:T(1024)}, f32[55552]{0:T(1024)S(1)}, u32[]{:S(2)}) copy-start(f32[55552]{0:T(1024)S(1)} %collective-permute-done.2) | copy-start | bytes 666628
  438.8 8.1 %collective-permute-start.3 = (f32[55552]{0:T(1024)S(1)}, f32[55552]{0:T(1024)}, u32[]{:S(2)}, u32[]{:S(2)}) collective-permute-start(f32[55552]{0:T(1024)S(1)} %collective-permute-done.2), channel_id=1, source_target_pairs={{0,15},{1,0},{2,1},{3,2},{4,3},{5,4},{6,5},{7,6},{8,7},{9,8},{10,9... | collective-permute-start | bytes 666632 | tf_op jit(solution)/shard_map/ppermute | solution.py:203
  446.9 11.3 %collective-permute-start.4 = (f32[55552]{0:T(1024)}, f32[55552]{0:T(1024)}, u32[]{:S(2)}, u32[]{:S(2)}) collective-permute-start(f32[55552]{0:T(1024)} %collective-permute-done.3), channel_id=1, source_target_pairs={{0,15},{1,0},{2,1},{3,2},{4,3},{5,4},{6,5},{7,6},{8,7},{9,8},{10,9... | collective-permute-start | bytes 666632 | tf_op jit(solution)/shard_map/ppermute | solution.py:203
  458.2 5.7 collective-permute-start.5
  463.9 12.7 %copy-start.20 = (f32[55552]{0:T(1024)}, f32[55552]{0:T(1024)S(1)}, u32[]{:S(2)}) copy-start(f32[55552]{0:T(1024)S(1)} %collective-permute-done.5) | copy-start | bytes 666628
  463.9 8.0 %collective-permute-start.6 = (f32[55552]{0:T(1024)S(1)}, f32[55552]{0:T(1024)}, u32[]{:S(2)}, u32[]{:S(2)}) collective-permute-start(f32[55552]{0:T(1024)S(1)} %collective-permute-done.5), channel_id=1, source_target_pairs={{0,15},{1,0},{2,1},{3,2},{4,3},{5,4},{6,5},{7,6},{8,7},{9,8},{10,9... | collective-permute-start | bytes 666632 | tf_op jit(solution)/shard_map/ppermute | solution.py:203
  471.9 8.5 %collective-permute-start.7 = (f32[55552]{0:T(1024)}, f32[55552]{0:T(1024)}, u32[]{:S(2)}, u32[]{:S(2)}) collective-permute-start(f32[55552]{0:T(1024)} %collective-permute-done.6), channel_id=1, source_target_pairs={{0,15},{1,0},{2,1},{3,2},{4,3},{5,4},{6,5},{7,6},{8,7},{9,8},{10,9... | collective-permute-start | bytes 666632 | tf_op jit(solution)/shard_map/ppermute | solution.py:203
  476.6 10.1 %copy-start.17 = (f32[55552]{0:T(1024)S(1)}, f32[55552]{0:T(1024)}, u32[]{:S(2)}) copy-start(f32[55552]{0:T(1024)} %copy-done.16) | copy-start | bytes 666628
  476.6 16.7 %copy-start.19 = (f32[55552]{0:T(1024)S(1)}, f32[55552]{0:T(1024)}, u32[]{:S(2)}) copy-start(f32[55552]{0:T(1024)} %copy-done.18) | copy-start | bytes 666628
  478.8 24.3 %copy-start.21 = (f32[55552]{0:T(1024)S(1)}, f32[55552]{0:T(1024)}, u32[]{:S(2)}) copy-start(f32[55552]{0:T(1024)} %copy-done.20) | copy-start | bytes 666628
  480.4 8.4 %collective-permute-start.8 = (f32[55552]{0:T(1024)}, f32[55552]{0:T(1024)S(1)}, u32[]{:S(2)}, u32[]{:S(2)}) collective-permute-start(f32[55552]{0:T(1024)} %collective-permute-done.7), channel_id=1, source_target_pairs={{0,15},{1,0},{2,1},{3,2},{4,3},{5,4},{6,5},{7,6},{8,7},{9,8},{10,9... | collective-permute-start | bytes 666632 | tf_op jit(solution)/shard_map/ppermute | solution.py:203
  488.8 8.0 %collective-permute-start.9 = (f32[55552]{0:T(1024)S(1)}, f32[55552]{0:T(1024)S(1)}, u32[]{:S(2)}, u32[]{:S(2)}) collective-permute-start(f32[55552]{0:T(1024)S(1)} %collective-permute-done.8), channel_id=1, source_target_pairs={{0,15},{1,0},{2,1},{3,2},{4,3},{5,4},{6,5},{7,6},{8,7},{9,8},{10,9... | collective-permute-start | bytes 666632 | tf_op jit(solution)/shard_map/ppermute | solution.py:203
  496.8 8.1 %collective-permute-start.10 = (f32[55552]{0:T(1024)S(1)}, f32[55552]{0:T(1024)S(1)}, u32[]{:S(2)}, u32[]{:S(2)}) collective-permute-start(f32[55552]{0:T(1024)S(1)} %collective-permute-done.9), channel_id=1, source_target_pairs={{0,15},{1,0},{2,1},{3,2},{4,3},{5,4},{6,5},{7,6},{8,7},{9,8},{10,9... | collective-permute-start | bytes 666632 | tf_op jit(solution)/shard_map/ppermute | solution.py:203
  504.9 8.1 %collective-permute-start.11 = (f32[55552]{0:T(1024)S(1)}, f32[55552]{0:T(1024)S(1)}, u32[]{:S(2)}, u32[]{:S(2)}) collective-permute-start(f32[55552]{0:T(1024)S(1)} %collective-permute-done.10), channel_id=1, source_target_pairs={{0,15},{1,0},{2,1},{3,2},{4,3},{5,4},{6,5},{7,6},{8,7},{9,8},{10,9... | collective-permute-start | bytes 666632 | tf_op jit(solution)/shard_map/ppermute | solution.py:203
  513.0 8.1 %collective-permute-start.12 = (f32[55552]{0:T(1024)S(1)}, f32[55552]{0:T(1024)S(1)}, u32[]{:S(2)}, u32[]{:S(2)}) collective-permute-start(f32[55552]{0:T(1024)S(1)} %collective-permute-done.11), channel_id=1, source_target_pairs={{0,15},{1,0},{2,1},{3,2},{4,3},{5,4},{6,5},{7,6},{8,7},{9,8},{10,9... | collective-permute-start | bytes 666632 | tf_op jit(solution)/shard_map/ppermute | solution.py:203
  521.1 8.1 %collective-permute-start.13 = (f32[55552]{0:T(1024)S(1)}, f32[55552]{0:T(1024)S(1)}, u32[]{:S(2)}, u32[]{:S(2)}) collective-permute-start(f32[55552]{0:T(1024)S(1)} %collective-permute-done.12), channel_id=1, source_target_pairs={{0,15},{1,0},{2,1},{3,2},{4,3},{5,4},{6,5},{7,6},{8,7},{9,8},{10,9... | collective-permute-start | bytes 666632 | tf_op jit(solution)/shard_map/ppermute | solution.py:203
  529.2 8.1 %collective-permute-start.14 = (f32[55552]{0:T(1024)S(1)}, f32[55552]{0:T(1024)S(1)}, u32[]{:S(2)}, u32[]{:S(2)}) collective-permute-start(f32[55552]{0:T(1024)S(1)} %collective-permute-done.13), channel_id=1, source_target_pairs={{0,15},{1,0},{2,1},{3,2},{4,3},{5,4},{6,5},{7,6},{8,7},{9,8},{10,9... | collective-permute-start | bytes 666632 | tf_op jit(solution)/shard_map/ppermute | solution.py:203
Sparse Core Ops, SparseCore 0:
  10.8 52.2 all-gather.1
  210.8 94.7 all-reduce.5
  309.8 106.4 all-reduce.3
